TPU v7x, 32 devices: a whole 2x2x4 slice. The times are simulated.
32 devices in a mesh: shard: 4 (over y, core), context: 2 (over x), tensor: 4 (over z).
Axes of the slice: x: 2, y: 2, z: 4, core: 2. Of those that a mesh axis runs over, the one named last changes fastest.
Arguments:
- block_input: bfloat16 [8192, 1536], P(('shard', 'context')), may hold values from -6 to 6
- norm_gain: float32 [1536], replicated, may hold values from 0.5 to 1.5
- w_z: bfloat16 [1536, 3072], P('shard', 'tensor'), may hold values from -0.15625 to 0.15625
- w_x: bfloat16 [1536, 3072], P('shard', 'tensor'), may hold values from -0.15625 to 0.15625
- w_bc: bfloat16 [1536, 256], P('shard'), may hold values from -0.15625 to 0.15625
- w_dt: bfloat16 [1536, 48], P('shard', 'tensor'), may hold values from -0.15625 to 0.15625
- conv_x_weight: float32 [4, 3072], P(None, 'tensor'), may hold values from -3 to 3
- conv_x_bias: float32 [3072], P('tensor'), may hold values from -1.5 to 1.5
- conv_bc_weight: float32 [4, 256], replicated, may hold values from -3 to 3
- conv_bc_bias: float32 [256], replicated, may hold values from -1.5 to 1.5
- dt_bias: float32 [48], P('tensor'), may hold values from -4 to -1
- a_log: float32 [48], P('tensor'), may hold values from -9 to 0
- d_skip: float32 [48], P('tensor'), may hold values from 0.5 to 1.5
- gate_gain: float32 [3072], P('tensor'), may hold values from 0.5 to 1.5
- w_out: bfloat16 [3072, 1536], P('tensor', 'shard'), may hold values from -0.109375 to 0.109375
- out_cotangent: bfloat16 [8192, 1536], P(('shard', 'context')), may hold values from -6 to 6
Outputs:
- block_output: bfloat16 [8192, 1536], P(('shard', 'context'))
- input_grad: float32 [8192, 1536], P(('shard', 'context'))
- grad_w_z: float32 [1536, 3072], P(('shard', 'context'), 'tensor')
- grad_w_x: float32 [1536, 3072], P(('shard', 'context'), 'tensor')
- grad_w_bc: float32 [1536, 256], P(('shard', 'context'))
- grad_w_dt: float32 [1536, 48], P(('shard', 'context'), 'tensor')
- grad_w_out: float32 [3072, 1536], P('tensor', ('shard', 'context'))
- grad_norm_gain: float32 [1536], replicated
- grad_conv_x_weight: float32 [4, 3072], P(None, 'tensor')
- grad_conv_x_bias: float32 [3072], P('tensor')
- grad_conv_bc_weight: float32 [4, 256], replicated
- grad_conv_bc_bias: float32 [256], replicated
- grad_dt_bias: float32 [48], P('tensor')
- grad_a_log: float32 [48], P('tensor')
- grad_d_skip: float32 [48], P('tensor')
- grad_gate_gain: float32 [3072], P('tensor')
All inputs are finite; a program needn't handle non-finite values.
Results may differ from a plain program's by a relative error of at most 0.0021.
The roundings to bfloat16 on the way count: a program that leaves them out, or rounds other values in their place, can miss the bound.
Values may be sent and summed in bfloat16 or wider, within the bound.
No kernel may reach another device: no remote copies, remote signals or barrier semaphores. Data moves between devices by JAX's collectives and lax.ppermute only.
A program may use at most 192 MiB of HBM per device.

v0:
```python
import jax
import jax.numpy as jnp
from jax import lax
from jax.sharding import PartitionSpec as P

HEADS = 48
HEAD_DIM = 64
STATE = 128
CONV = 4
GROUP = 256
epsilon = 1e-05
precise = lax.Precision.HIGHEST


def shifted(shard, axis, by):
    length = lax.axis_size(axis)
    pairs = [(i, i + by) for i in range(length) if 0 <= i + by < length]
    return lax.ppermute(shard, axis, pairs)


def prefix(value, axis, join, neutral, backward):
    count, mine = (lax.axis_size(axis), lax.axis_index(axis))
    pieces = jax.tree.map(lambda part: lax.all_gather(part, axis), value)
    if backward:
        pieces = jax.tree.map(lambda part: part[::-1], pieces)
        mine = count - 1 - mine
    running = jax.tree.map(
        lambda part, zero: jnp.full_like(part, 0) + jnp.asarray(zero, part.dtype), value, neutral
    )

    def hop(position, running):
        longer = join(running, jax.tree.map(lambda part: part[position], pieces))
        return jax.tree.map(lambda new, old: jnp.where(position < mine, new, old), longer, running)

    return lax.fori_loop(0, count - 1, hop, running)


def silu_slope(value):
    sigma = jax.nn.sigmoid(value)
    return sigma * (1.0 + value * (1.0 - sigma))


def group_states(x_conv, step_size, decay_rate, b_mat, span):
    length, heads, width = x_conv.shape
    count = length // span
    log_step = (-step_size * decay_rate[None, :]).reshape(count, span, heads)
    cum_log = jnp.cumsum(log_step, axis=1)
    x_step = (x_conv * step_size[:, :, None]).reshape(count, span, heads, width)
    tail = jnp.exp(cum_log[:, -1:, :] - cum_log)
    states = jnp.einsum(
        "cqhp,cqn->chpn",
        x_step * tail[:, :, :, None],
        b_mat.reshape(count, span, -1),
        precision=precise,
    )
    return (cum_log, x_step, states)


def summarize(cum_log, states):
    totals = cum_log[:, -1, :]

    def advance(carry, item):
        total, state = item
        return (jnp.exp(total)[:, None, None] * carry + state, carry)

    final, enter = lax.scan(advance, jnp.zeros(states.shape[1:], jnp.float32), (totals, states))
    return (enter, jnp.sum(totals, axis=0), final)


def entry_scale(cum_log):
    totals = cum_log[:, -1, :]
    return jnp.exp(jnp.cumsum(totals, axis=0) - totals)


def group_output(cum_log, x_step, b_mat, c_mat, enter):
    count, span, heads, width = x_step.shape
    b_view = b_mat.reshape(count, span, -1)
    c_view = c_mat.reshape(count, span, -1)
    scores = jnp.einsum("ctn,csn->cts", c_view, b_view, precision=precise)
    cum_heads = jnp.transpose(cum_log, (0, 2, 1))
    gaps = cum_heads[:, :, :, None] - cum_heads[:, :, None, :]
    lower = jnp.arange(span)[:, None] >= jnp.arange(span)[None, :]
    decay = jnp.where(lower, jnp.exp(jnp.minimum(gaps, 0.0)), 0.0)
    inner = jnp.einsum("chts,cshp->cthp", decay * scores[:, None], x_step, precision=precise)
    outer = (
        jnp.einsum("ctn,chpn->cthp", c_view, enter, precision=precise)
        * jnp.exp(cum_log)[:, :, :, None]
    )
    return (inner + outer).reshape(count * span, heads, width)


def ssd_local(x_conv, step_size, decay_rate, b_mat, c_mat, s_in):
    span = min(GROUP, x_conv.shape[0])
    cum_log, x_step, states = group_states(x_conv, step_size, decay_rate, b_mat, span)
    enter, log_decay, s_local = summarize(cum_log, states)
    before = entry_scale(cum_log)
    enter = enter + before[:, :, None, None] * s_in[None]
    return (group_output(cum_log, x_step, b_mat, c_mat, enter), log_decay, s_local)


def combine_carry(earlier, later):
    return (earlier[0] + later[0], earlier[1] * jnp.exp(later[0])[:, None, None] + later[1])


def conv_apply(padded, conv_weight, conv_bias, length):
    total = conv_bias[None, :] + conv_weight[0] * padded[0:length]
    for offset in range(1, CONV):
        total = total + conv_weight[offset] * padded[offset : offset + length]
    return total


def conv_transpose(grad_pre, conv_weight):
    total = jnp.pad(conv_weight[0] * grad_pre, ((0, CONV - 1), (0, 0)))
    for offset in range(1, CONV):
        total = total + jnp.pad(
            conv_weight[offset] * grad_pre, ((offset, CONV - 1 - offset), (0, 0))
        )
    return total


def shards(
    block_input,
    norm_gain,
    w_z,
    w_x,
    w_bc,
    w_dt,
    conv_x_weight,
    conv_x_bias,
    conv_bc_weight,
    conv_bc_bias,
    dt_bias,
    a_log,
    d_skip,
    gate_gain,
    w_out,
    out_cotangent,
):
    full_z, full_x, full_bc, full_dt, full_out = (
        lax.all_gather(w_z, "shard", axis=0, tiled=True),
        lax.all_gather(w_x, "shard", axis=0, tiled=True),
        lax.all_gather(w_bc, "shard", axis=0, tiled=True),
        lax.all_gather(w_dt, "shard", axis=0, tiled=True),
        lax.all_gather(w_out, "shard", axis=1, tiled=True),
    )
    length = block_input.shape[0]
    local_inner = w_z.shape[1]
    heads_here = w_dt.shape[1]
    inner_width = HEADS * HEAD_DIM
    x_float = block_input.astype(jnp.float32)
    inverse = lax.rsqrt(jnp.mean(x_float * x_float, axis=1, keepdims=True) + epsilon)
    normed = (x_float * inverse * norm_gain).astype(jnp.bfloat16)
    z_part = jnp.dot(normed, full_z, preferred_element_type=jnp.float32)
    x_raw = jnp.dot(normed, full_x, preferred_element_type=jnp.float32).astype(jnp.bfloat16)
    bc_raw = jnp.dot(normed, full_bc, preferred_element_type=jnp.float32).astype(jnp.bfloat16)
    dt_raw = jnp.dot(normed, full_dt, preferred_element_type=jnp.float32)
    conv_in = jnp.concatenate([x_raw, bc_raw], axis=1)
    edge = shifted(conv_in[length - CONV + 1 :], "context", 1)
    padded = jnp.concatenate([edge, conv_in], axis=0).astype(jnp.float32)
    conv_weight = jnp.concatenate([conv_x_weight, conv_bc_weight], axis=1)
    conv_bias = jnp.concatenate([conv_x_bias, conv_bc_bias])
    pre = conv_apply(padded, conv_weight, conv_bias, length)
    act = jax.nn.silu(pre)
    x_conv = act[:, :local_inner].reshape(length, heads_here, HEAD_DIM)
    b_mat = act[:, local_inner : local_inner + STATE]
    c_mat = act[:, local_inner + STATE :]
    step_size = jax.nn.softplus(dt_raw + dt_bias)
    decay_rate = jnp.exp(a_log)
    span = min(GROUP, length)
    cum_log, x_step, states = group_states(x_conv, step_size, decay_rate, b_mat, span)
    enter, log_decay, s_local = summarize(cum_log, states)
    identity = (jnp.zeros_like(log_decay), jnp.zeros_like(s_local))
    s_in = prefix((log_decay, s_local), "context", combine_carry, identity, False)[1]
    before = entry_scale(cum_log)
    enter = enter + before[:, :, None, None] * s_in[None]
    ssd_out = group_output(cum_log, x_step, b_mat, c_mat, enter)
    mixer = (ssd_out + d_skip[None, :, None] * x_conv).reshape(length, local_inner)
    gate_value = jax.nn.silu(z_part)
    gated = mixer * gate_value
    square_sum = lax.psum(jnp.sum(gated * gated, axis=1), "tensor")
    gate_inverse = lax.rsqrt(square_sum[:, None] / inner_width + epsilon)
    gated_out = (gated * gate_inverse * gate_gain).astype(jnp.bfloat16)
    out_part = jnp.dot(gated_out, full_out, preferred_element_type=jnp.float32)
    out_total = lax.psum(out_part, "tensor")
    block_output = (x_float + out_total).astype(jnp.bfloat16)
    grad_gated_out = jnp.einsum(
        "td,kd->tk", out_cotangent, full_out, preferred_element_type=jnp.float32
    )
    grad_w_out = jnp.einsum(
        "tk,td->kd", gated_out, out_cotangent, preferred_element_type=jnp.float32
    )
    scaled = gate_gain * grad_gated_out
    row_terms = lax.psum(jnp.sum(scaled * gated, axis=1), "tensor")
    grad_gated = gate_inverse * scaled - gated * gate_inverse * gate_inverse * gate_inverse * (
        row_terms[:, None] / inner_width
    )
    grad_gate_gain = jnp.sum(grad_gated_out * gated * gate_inverse, axis=0)
    grad_mixer = grad_gated * gate_value
    grad_z = (grad_gated * mixer * silu_slope(z_part)).astype(jnp.bfloat16)
    grad_heads = grad_mixer.reshape(length, heads_here, HEAD_DIM)
    grad_d_skip = jnp.sum(grad_heads * x_conv, axis=(0, 2))
    count = length // span
    weighted = (
        grad_heads.reshape(count, span, heads_here, HEAD_DIM)
        * (jnp.exp(cum_log) * before[:, None, :])[:, :, :, None]
    )
    own_grad = jnp.einsum(
        "cqhp,cqn->hpn", weighted, c_mat.reshape(count, span, STATE), precision=precise
    )
    carried = prefix((log_decay, own_grad), "context", combine_carry, identity, True)[1]
    grad_decay = jnp.sum(carried * s_in, axis=(1, 2)) * jnp.exp(log_decay)
    unused_out, pullback = jax.vjp(ssd_local, x_conv, step_size, decay_rate, b_mat, c_mat, s_in)
    grad_xc, grad_step, grad_rate, grad_b, grad_c, unused_state = pullback(
        (grad_heads, grad_decay, carried)
    )
    grad_xc = grad_xc + d_skip[None, :, None] * grad_heads
    grad_bc = lax.psum(jnp.concatenate([grad_b, grad_c], axis=1), "tensor")
    grad_act = jnp.concatenate([grad_xc.reshape(length, local_inner), grad_bc], axis=1)
    grad_pre = grad_act * silu_slope(pre)
    grad_conv_bias = jnp.sum(grad_pre, axis=0)
    grad_conv_weight = jnp.stack(
        [jnp.sum(grad_pre * padded[offset : offset + length], axis=0) for offset in range(CONV)]
    )
    grad_padded = conv_transpose(grad_pre, conv_weight)
    back_edge = shifted(grad_padded[: CONV - 1], "context", -1)
    grad_conv_in = grad_padded[CONV - 1 :] + jnp.pad(back_edge, ((length - CONV + 1, 0), (0, 0)))
    grad_x_raw = grad_conv_in[:, :local_inner].astype(jnp.bfloat16)
    grad_bc_raw = grad_conv_in[:, local_inner:].astype(jnp.bfloat16)
    slope = jax.nn.sigmoid(dt_raw + dt_bias)
    grad_dt_bias = jnp.sum(grad_step * slope, axis=0)
    grad_dt_raw = (grad_step * slope).astype(jnp.bfloat16)
    grad_a_log = grad_rate * decay_rate
    partial_normed = (
        jnp.einsum("tk,dk->td", grad_z, full_z, preferred_element_type=jnp.float32)
        + jnp.einsum("tk,dk->td", grad_x_raw, full_x, preferred_element_type=jnp.float32)
        + jnp.einsum("tk,dk->td", grad_dt_raw, full_dt, preferred_element_type=jnp.float32)
    )
    grad_normed = lax.psum(partial_normed, "tensor") + jnp.einsum(
        "tk,dk->td", grad_bc_raw, full_bc, preferred_element_type=jnp.float32
    )
    scaled_in = norm_gain * grad_normed
    input_grad = (
        out_cotangent.astype(jnp.float32)
        + inverse * scaled_in
        - x_float
        * inverse
        * inverse
        * inverse
        * jnp.mean(scaled_in * x_float, axis=1, keepdims=True)
    )
    grad_norm_gain = jnp.sum(grad_normed * x_float * inverse, axis=0)
    grad_w_z = jnp.einsum("td,tk->dk", normed, grad_z, preferred_element_type=jnp.float32)
    grad_w_x = jnp.einsum("td,tk->dk", normed, grad_x_raw, preferred_element_type=jnp.float32)
    grad_w_bc = jnp.einsum("td,tk->dk", normed, grad_bc_raw, preferred_element_type=jnp.float32)
    grad_w_dt = jnp.einsum("td,tk->dk", normed, grad_dt_raw, preferred_element_type=jnp.float32)
    summed_z, summed_x, summed_bc, summed_dt, summed_out = (
        lax.psum_scatter(grad_w_z, ("shard", "context"), scatter_dimension=0, tiled=True),
        lax.psum_scatter(grad_w_x, ("shard", "context"), scatter_dimension=0, tiled=True),
        lax.psum_scatter(grad_w_bc, ("shard", "context"), scatter_dimension=0, tiled=True),
        lax.psum_scatter(grad_w_dt, ("shard", "context"), scatter_dimension=0, tiled=True),
        lax.psum_scatter(grad_w_out, ("shard", "context"), scatter_dimension=1, tiled=True),
    )
    (
        sum_norm_gain,
        sum_conv_x_weight,
        sum_conv_x_bias,
        sum_conv_bc_weight,
        sum_conv_bc_bias,
        sum_dt_bias,
        sum_a_log,
        sum_d_skip,
        sum_gate_gain,
    ) = lax.psum(
        (
            grad_norm_gain,
            grad_conv_weight[:, :local_inner],
            grad_conv_bias[:local_inner],
            grad_conv_weight[:, local_inner:],
            grad_conv_bias[local_inner:],
            grad_dt_bias,
            grad_a_log,
            grad_d_skip,
            grad_gate_gain,
        ),
        ("shard", "context"),
    )
    return (
        block_output,
        input_grad,
        summed_z,
        summed_x,
        summed_bc,
        summed_dt,
        summed_out,
        sum_norm_gain,
        sum_conv_x_weight,
        sum_conv_x_bias,
        sum_conv_bc_weight,
        sum_conv_bc_bias,
        sum_dt_bias,
        sum_a_log,
        sum_d_skip,
        sum_gate_gain,
    )


def solution(mesh):
    in_specs = (
        P(("shard", "context"), None),
        P(),
        P("shard", "tensor"),
        P("shard", "tensor"),
        P("shard", None),
        P("shard", "tensor"),
        P(None, "tensor"),
        P("tensor"),
        P(),
        P(),
        P("tensor"),
        P("tensor"),
        P("tensor"),
        P("tensor"),
        P("tensor", "shard"),
        P(("shard", "context"), None),
    )
    out_specs = (
        P(("shard", "context"), None),
        P(("shard", "context"), None),
        P(("shard", "context"), "tensor"),
        P(("shard", "context"), "tensor"),
        P(("shard", "context"), None),
        P(("shard", "context"), "tensor"),
        P("tensor", ("shard", "context")),
        P(),
        P(None, "tensor"),
        P("tensor"),
        P(),
        P(),
        P("tensor"),
        P("tensor"),
        P("tensor"),
        P("tensor"),
    )
    return jax.shard_map(shards, mesh=mesh, in_specs=in_specs, out_specs=out_specs, check_vma=False)
```

profile of v0, /device:TPU:0, one launch (start us, length us, event | category | flops | bytes accessed | tf_op | source)
XLA Modules:
  0.0 1078.0 jit_solution(2125863007557966451)
XLA Ops:
  12.7 6.3 all_gather.37
  27.7 12.3 %all_gather.36 = bf16[1536,256]{1,0:T(8,128)(2,1)S(1)} all-gather(bf16[384,256]{1,0:T(8,128)(2,1)S(1)} %copy-done.50), channel_id=1, replica_groups=mesh['shard'=4,'context'=2,'tensor'=4] {'shard'}, dimensions={0}, use_global_device_ids=true | all-gather | bytes 983040 | tf_op jit(solution)/shard_map/all_gather | solution.py:142
  40.8 3.7 convolution_convert_fusion.1
  46.7 4.9 all-reduce.8
  52.2 4.4 convolution_convert_fusion
  57.7 4.5 collective-permute-start
  73.8 5.4 fusion.39
  83.2 5.2 reshape.251
  92.5 6.4 fusion.53
  100.3 7.7 while.59
  116.2 10.8 all-gather.1
  133.1 14.4 %bitcast_add_fusion.4 = f32[4,256,12,64]{1,3,2,0:T(8,128)S(1)} fusion(f32[4,256,12,64]{1,3,2,0:T(8,128)S(1)} %fusion.67, f32[4,256,256]{2,1,0:T(8,128)S(1)} %fusion.129, f32[4,12,256]{2,1,0:T(8,128)S(1)} %copy-done.32, pred[256,256]{1,0:T(8,128)(4,1)S(1)} %copy-done.53, f32[4,256,12,64]{1,0,3,2:T(4,128)S(1)} %copy-done.6, f32[4,256,12]{1,2,0:T(8,128)S(1)} %copy-done.43, ...), kind=kOutput, calls=%fused_computation.75 | convolution fusion | flops 2430861312 | bytes 10698752 | tf_op jit(solution)/shard_map/chts,cshp->cthp/dot_general | solution.py:84
  151.9 7.9 multiply_reduce_fusion.10
  159.9 11.7 %psum.98 = f32[1024]{0:T(1024)S(1)} all-reduce(f32[1024]{0:T(1024)S(1)} %get-tuple-element.403), channel_id=1, replica_groups=mesh['shard'=4,'context'=2,'tensor'=4] {'tensor'}, use_global_device_ids=true, to_apply=%region_8.9 | all-reduce | flops 1024 | bytes 8192 | tf_op jit(solution)/shard_map/psum | solution.py:180
  171.6 8.6 multiply_reduce_fusion.4
  180.2 8.7 psum.100
  188.9 8.5 multiply_reduce_fusion.5
  200.4 6.9 multiply_reduce_fusion.11
  209.7 5.2 mul.624
  214.9 4.7 fusion.86
  219.6 8.7 all-gather.2
  230.2 14.7 %while.60 = (s32[]{:T(128)}, f32[12,64,128]{2,1,0:T(8,128)S(1)}, f32[4,12,64,128]{3,2,1,0:T(8,128)}, f32[4,12]{1,0:T(4,128)}, f32[4,12,1,1]{1,3,2,0:T(1,128)}, /...) while((s32[]{:T(128)}, f32[12,64,128]{2,1,0:T(8,128)S(1)}, ...), condition=%wide.region_13.14_spmd.clone, body=%wide.region_12.13_spmd.clone.sunk | while | flops 393219 | bytes 1967968 | solution.py:66
  248.8 18.7 %while.58 = (s32[]{:T(128)}, f32[12,64,128]{2,1,0:T(8,128)S(1)}, f32[4,12]{1,0:T(4,128)}, f32[4,12,64,128]{3,2,1,0:T(8,128)}, f32[4,12,64,128]{3,2,1,0:T(8,128)}...) while((s32[]{:T(128)}, f32[12,64,128]{2,1,0:T(8,128)S(1)}, ...), condition=%wide.region_16.17_spmd, body=%wide.region_14.16_spmd.sunk | while | flops 393219 | bytes 2359869 | solution.py:66
  267.5 6.0 multiply_reduce_fusion.6
  273.6 5.3 fusion.83
  278.9 20.5 %fusion.60 = (f32[4,12,256]{2,1,0:T(8,128)S(1)}, f32[4,12,256]{2,1,0:T(8,128)}, f32[4,256,256]{2,1,0:T(8,128)S(1)}) fusion(f32[4,12,256]{2,1,0:T(8,128)S(1)} %copy-done.33, f32[4,256,256]{2,1,0:T(8,128)S(1)} %copy-done.40, pred[256,256]{1,0:T(8,128)(4,1)S(1)} %copy-done.54, f32[4,256,12,64]{1,0,3,2:T(4,128)S(1)} %copy-done.7, ...), kind=kOutput, calls=%fused_computation.106 | convolution fusion | flops 2463604736 | bytes 8650752 | tf_op jit(solution)/shard_map/transpose(jvp(chts,cshp->cthp))/dot_general | solution.py:84
  299.4 6.2 fusion.80
  308.7 12.6 %bitcast_add_fusion.3 = f32[4,256,12,64]{1,3,2,0:T(8,128)} fusion(f32[4,256,12,64]{1,3,2,0:T(8,128)S(1)} %get-tuple-element.434, f32[4,256,256]{2,1,0:T(8,128)S(1)} %copy-done.40, f32[4,12,256]{2,1,0:T(8,128)S(1)} %copy-done.33, pred[256,256]{1,0:T(8,128)(4,1)S(1)} %copy-done.54, f32[4,256,12,64]{1,0,3,2:T(4,128)S(1)} %copy-done.8, ...), kind=kOutput, calls=%fused_computation.71 | convolution fusion | flops 2430074880 | bytes 10649600 | tf_op jit(solution)/shard_map/transpose(jvp(chts,cshp->cthp))/dot_general | solution.py:84
  335.8 9.9 reduce-window.16
  356.0 3.9 fusion.109
  359.9 3.7 fusion.111
  363.7 6.8 fusion.121
  370.5 4.7 fusion.130
  375.2 8.6 all-reduce.14.cloned.1.call-done
  383.8 12.4 %multiply_reduce_fusion.3 = (f32[1024]{0:T(1024)S(1)}, f32[1024]{0:T(1024)S(1)}, f32[1024]{0:T(1024)S(1)}, f32[1024]{0:T(1024)S(1)}, f32[1024]{0:T(1024)S(1)}, /*index=5*/f32[1024,1024]{0,1:T(8,128)S(1)}) fusion(f32[1027,1024]{0,1:T(8,128)} %copy-done, f32[1024,1024]{0,1:T(8,128)} %get-tuple-element.406, f32[1024,256]{0,1:T(8,128)} %all-reduce.14.cloned.1.call-done, ...), kind=kLoop, calls=%fused_computation.65 | loop fusion | flops 18869248 | bytes 29380608 | tf_op jit(solution)/shard_map/reduce_sum | solution.py:222
  402.1 9.5 pad_add_fusion
  411.6 7.0 collective-permute-done.1
  423.1 8.1 add_add_fusion
  436.4 8.0 fusion.120
  444.4 5.7 fusion.131
  450.2 5.7 fusion.77
  458.7 397.3 %all-reduce.16.cloned.1.call-done = (f32[1024,1536]{1,0:T(8,128)}, f32[1024,1536]{1,0:T(8,128)}) async-done(((f32[1024,1536]{1,0:T(8,128)}, f32[1024,1536]{1,0:T(8,128)}), (f32[1024,1536]{1,0:T(8,128)}, f32[1024,1536]{1,0:T(8,128)})) %all-reduce.16.cloned.1.call-update) | async-done | bytes 12582928 | tf_op jit(solution)/shard_map/psum | solution.py:184
  856.0 8.2 fusion.27
  864.2 25.9 %all-reduce.9 = (f32[1536]{0:T(1024)}, f32[4,768]{1,0:T(4,128)}, f32[768]{0:T(1024)}, f32[4,256]{1,0:T(4,128)}, f32[256]{0:T(256)}, /*index=5*/f32[12]{0:T(128)}, f32[12]{0:T(128)}, f32[12]{0:T(128)}, f32[768]{0:T(1024)}) all-reduce(f32[1536]{0:T(1024)S(1)} %get-tuple-element.332, ...), channel_id=1, replica_groups=mesh['shard'=4,'context'=2,'tensor'=4] {'shard','context'}, use_global_device_ids=true, to_apply=%region_38.39 | all-reduce | flops 7460 | bytes 59680 | tf_op jit(solution)/shard_map/psum | solution.py:273
  890.1 9.2 fusion.22
  899.3 56.2 %reduce-scatter.14.cloned.1.call-done = f32[768,192]{0,1:T(8,128)} async-done(((f32[768,1536]{0,1:T(8,128)}), f32[768,192]{0,1:T(8,128)}) %reduce-scatter.14.cloned.1.call-update) | async-done | bytes 589840 | tf_op jit(solution)/shard_map/reduce_scatter | solution.py:261
  955.5 57.8 %reduce-scatter.8.cloned.1.call-done = f32[192,768]{1,0:T(8,128)} async-done(((f32[1536,768]{1,0:T(8,128)}), f32[192,768]{1,0:T(8,128)}) %reduce-scatter.8.cloned.1.call-update) | async-done | bytes 589840 | tf_op jit(solution)/shard_map/reduce_scatter | solution.py:257
  1013.3 57.7 %reduce-scatter.10.cloned.1.call-done = f32[192,768]{1,0:T(8,128)} async-done(((f32[1536,768]{1,0:T(8,128)}), f32[192,768]{1,0:T(8,128)}) %reduce-scatter.10.cloned.1.call-update) | async-done | bytes 589840 | tf_op jit(solution)/shard_map/reduce_scatter | solution.py:258
  (373 shorter events, 155.8 us)
Async XLA Ops:
  7.2 11.9 %copy-start.1 = (bf16[1024,1536]{1,0:T(8,128)(2,1)S(1)}, bf16[1024,1536]{1,0:T(8,128)(2,1)}, u32[]{:S(2)}) copy-start(bf16[1024,1536]{1,0:T(8,128)(2,1)} %param.22) | copy-start | bytes 9437188
  7.2 11.8 %copy-start.90 = (f32[12]{0:T(128)S(1)}, f32[12]{0:T(128)}, u32[]{:S(2)}) copy-start(f32[12]{0:T(128)} %param.33) | copy-start | bytes 148
  7.2 11.8 %copy-start.51 = (f32[1536]{0:T(1024)S(1)}, f32[1536]{0:T(1024)}, u32[]{:S(2)}) copy-start(f32[1536]{0:T(1024)} %param.23) | copy-start | bytes 18436
  7.2 45.0 %all-gather.7.cloned.1.call-start = ((), (), s32[]{:S(2)}) async-start(), calls=%async_computation.5 | async-start | bytes 2949120 | tf_op jit(solution)/shard_map/all_gather | solution.py:141
  8.0 144.0 %all-gather.9.cloned.1.call-start = ((), (), s32[]{:S(2)}) async-start(), calls=%async_computation.6 | async-start | bytes 2949120 | tf_op jit(solution)/shard_map/all_gather | solution.py:140
  8.7 162.9 %all-gather.11.cloned.1.call-start = ((), (), s32[]{:S(2)}) async-start(), calls=%async_computation.7 | async-start | bytes 2949120 | tf_op jit(solution)/shard_map/all_gather | solution.py:144
  9.4 374.3 %all-reduce.14.cloned.1.call-start = ((), (), s32[]{:S(2)}) async-start(), calls=%async_computation.8 | async-start | bytes 2097152 | tf_op jit(solution)/shard_map/psum | solution.py:217
  26.5 19.9 %copy-start.85 = (f32[12]{0:T(128)}, f32[12]{0:T(128)S(1)}, u32[]{:S(2)}) copy-start(f32[12]{0:T(128)S(1)} %get-tuple-element.342) | copy-start | bytes 148
  27.6 16.9 %copy-start.71 = (f32[4,768]{1,0:T(4,128)S(1)}, f32[4,768]{1,0:T(4,128)}, u32[]{:S(2)}) copy-start(f32[4,768]{1,0:T(4,128)} %param.28) | copy-start | bytes 36868
  27.6 16.9 %copy-start.81 = (f32[4,256]{1,0:T(4,128)S(1)}, f32[4,256]{1,0:T(4,128)}, u32[]{:S(2)}) copy-start(f32[4,256]{1,0:T(4,128)} %param.30) | copy-start | bytes 12292
  27.6 17.6 %copy-start.92 = (u32[32]{0:T(128)S(1)}, u32[32]{0:T(128)}, u32[]{:S(2)}) copy-start(u32[32]{0:T(128)} %constant.163) | copy-start | bytes 388
  27.6 24.6 %copy-start.4 = (bf16[1024,1536]{1,0:T(8,128)(2,1)S(1)}, bf16[1024,1536]{1,0:T(8,128)(2,1)}, u32[]{:S(2)}) copy-start(bf16[1024,1536]{1,0:T(8,128)(2,1)} %copy-done.3) | copy-start | bytes 9437188
  45.2 28.5 %copy-start.59 = (f32[1,1024]{1,0:T(1,128)}, f32[1,1024]{1,0:T(1,128)S(1)}, u32[]{:S(2)}) copy-start(f32[1,1024]{1,0:T(1,128)S(1)} %get-tuple-element.424) | copy-start | bytes 12292
  52.2 10.0 copy-start.82
  52.2 10.0 copy-start.84
  52.2 13.5 %copy-start.88 = (f32[12]{0:T(128)S(1)}, f32[12]{0:T(128)}, u32[]{:S(2)}) copy-start(f32[12]{0:T(128)} %param.34) | copy-start | bytes 148
  57.7 13.2 %collective-permute-start = (bf16[3,1024]{0,1:T(8,128)(2,1)}, bf16[3,1024]{0,1:T(8,128)(2,1)}, u32[]{:S(2)}, u32[]{:S(2)}) collective-permute-start(bf16[3,1024]{0,1:T(8,128)(2,1)} %pad_maximum_fusion.1), channel_id=1, source_target_pairs={{0,4},{1,5},{2,6},{3,7},{8,12},{9,13},{10,14},{11,15},{16,20},{17,... | collective-permute-start | bytes 18440 | tf_op jit(solution)/shard_map/ppermute | solution.py:18
  67.2 121.8 %copy-start.57 = (f32[768]{0:T(1024)}, f32[768]{0:T(1024)S(1)}, u32[]{:S(2)}) copy-start(f32[768]{0:T(1024)S(1)} %mul.593) | copy-start | bytes 9220
  108.0 19.9 %copy-start.77 = (f32[12]{0:T(128)S(1)}, f32[12]{0:T(128)}, u32[]{:S(2)}) copy-start(f32[12]{0:T(128)} %get-tuple-element.429) | copy-start | bytes 148
  116.2 14.2 %copy-start.23 = (f32[4,256,128,1]{2,1,3,0:T(8,128)S(1)}, f32[4,256,128,1]{2,1,3,0:T(8,128)}, u32[]{:S(2)}) copy-start(f32[4,256,128,1]{2,1,3,0:T(8,128)} %copy.238) | copy-start | bytes 1572868
  116.2 14.2 %copy-start.26 = (f32[4,12,64,128]{3,2,1,0:T(8,128)S(1)}, f32[4,12,64,128]{3,2,1,0:T(8,128)}, u32[]{:S(2)}) copy-start(f32[4,12,64,128]{3,2,1,0:T(8,128)} %get-tuple-element.280) | copy-start | bytes 4718596
  128.0 72.4 %copy-start.16 = (f32[12,64,128]{2,1,0:T(8,128)}, f32[12,64,128]{2,1,0:T(8,128)S(1)}, u32[]{:S(2)}) copy-start(f32[12,64,128]{2,1,0:T(8,128)S(1)} %fusion.102) | copy-start | bytes 1179652
  130.3 17.2 %copy-start.39 = (f32[4,256,256]{2,1,0:T(8,128)}, f32[4,256,256]{2,1,0:T(8,128)S(1)}, u32[]{:S(2)}) copy-start(f32[4,256,256]{2,1,0:T(8,128)S(1)} %fusion.129) | copy-start | bytes 3145732
  171.5 17.4 %copy-start.68 = (f32[1024]{0:T(1024)}, f32[1024]{0:T(1024)S(1)}, u32[]{:S(2)}) copy-start(f32[1024]{0:T(1024)S(1)} %add_rsqrt_fusion) | copy-start | bytes 12292
  214.9 15.3 %copy-start.9 = (f32[12,64,128]{2,1,0:T(8,128)S(1)}, f32[12,64,128]{2,1,0:T(8,128)}, u32[]{:S(2)}) copy-start(f32[12,64,128]{2,1,0:T(8,128)} %custom-call.1) | copy-start | bytes 1179652
  230.2 14.8 %copy-start.78 = (f32[12]{0:T(128)S(1)}, f32[12]{0:T(128)}, u32[]{:S(2)}) copy-start(f32[12]{0:T(128)} %get-tuple-element.429) | copy-start | bytes 148
  278.9 20.5 %copy-start.13 = (f32[4,12,64,128]{3,2,1,0:T(8,128)S(1)}, f32[4,12,64,128]{3,2,1,0:T(8,128)}, u32[]{:S(2)}) copy-start(f32[4,12,64,128]{3,2,1,0:T(8,128)} %get-tuple-element.666) | copy-start | bytes 4718596
  278.9 20.5 %copy-start.17 = (f32[12,64,128]{2,1,0:T(8,128)S(1)}, f32[12,64,128]{2,1,0:T(8,128)}, u32[]{:S(2)}) copy-start(f32[12,64,128]{2,1,0:T(8,128)} %copy-done.16) | copy-start | bytes 1179652
  278.9 20.5 %copy-start.44 = (f32[4,256,12]{1,2,0:T(8,128)S(1)}, f32[4,256,12]{1,2,0:T(8,128)}, u32[]{:S(2)}) copy-start(f32[4,256,12]{1,2,0:T(8,128)} %get-tuple-element.421) | copy-start | bytes 147460
  299.4 22.0 %copy-start.27 = (f32[4,256,256]{2,1,0:T(8,128)}, f32[4,256,256]{2,1,0:T(8,128)S(1)}, u32[]{:S(2)}) copy-start(f32[4,256,256]{2,1,0:T(8,128)S(1)} %get-tuple-element.331) | copy-start | bytes 3145732
  308.7 12.7 %copy-start.22 = (f32[4,256,128]{2,1,0:T(8,128)S(1)}, f32[4,256,128]{2,1,0:T(8,128)}, u32[]{:S(2)}) copy-start(f32[4,256,128]{2,1,0:T(8,128)} %copy.202) | copy-start | bytes 1572868
  326.1 8.6 copy-start.46
  333.9 123.0 %reduce-scatter.16.cloned.1.call-start = ((), (), s32[]{:S(2)}) async-start(), calls=%async_computation.13 | async-start | bytes 884736
  363.6 492.4 %all-reduce.16.cloned.1.call-start = ((), (), s32[]{:S(2)}) async-start(), calls=%async_computation.14 | async-start | bytes 25165824 | tf_op jit(solution)/shard_map/psum | solution.py:184
  370.5 13.3 %copy-start.19 = (f32[1024,768]{0,1:T(8,128)S(1)}, f32[1024,768]{0,1:T(8,128)}, u32[]{:S(2)}) copy-start(f32[1024,768]{0,1:T(8,128)} %fusion.40) | copy-start | bytes 9437188
  383.7 12.4 %copy-start.60 = (f32[1,1024]{1,0:T(1,128)S(1)}, f32[1,1024]{1,0:T(1,128)}, u32[]{:S(2)}) copy-start(f32[1,1024]{1,0:T(1,128)} %copy-done.59) | copy-start | bytes 12292
  383.8 12.4 %copy-start.62 = (f32[1,1024]{1,0:T(1,128)S(1)}, f32[1,1024]{1,0:T(1,128)}, u32[]{:S(2)}) copy-start(f32[1,1024]{1,0:T(1,128)} %get-tuple-element.425) | copy-start | bytes 12292
  383.8 12.4 %copy-start.64 = (f32[1,1024]{1,0:T(1,128)S(1)}, f32[1,1024]{1,0:T(1,128)}, u32[]{:S(2)}) copy-start(f32[1,1024]{1,0:T(1,128)} %get-tuple-element.426) | copy-start | bytes 12292
  383.8 12.4 %copy-start.66 = (f32[1,1024]{1,0:T(1,128)S(1)}, f32[1,1024]{1,0:T(1,128)}, u32[]{:S(2)}) copy-start(f32[1,1024]{1,0:T(1,128)} %get-tuple-element.427) | copy-start | bytes 12292
  400.8 17.8 %collective-permute-start.1 = (f32[3,1024]{0,1:T(8,128)S(1)}, f32[3,1024]{0,1:T(8,128)S(1)}, u32[]{:S(2)}, u32[]{:S(2)}) collective-permute-start(f32[3,1024]{0,1:T(8,128)S(1)} %pad_add_fusion.1), channel_id=1, source_target_pairs={{4,0},{5,1},{6,2},{7,3},{12,8},{13,9},{14,10},{15,11},{20,16},{21,... | collective-permute-start | bytes 36872 | tf_op jit(solution)/shard_map/ppermute | solution.py:18
  411.6 11.5 %copy-start.34 = (bf16[1536,768]{1,0:T(8,128)(2,1)S(1)}, bf16[1536,768]{1,0:T(8,128)(2,1)}, u32[]{:S(2)}) copy-start(bf16[1536,768]{1,0:T(8,128)(2,1)} %all-gather.7.cloned.1.call-done) | copy-start | bytes 7077892
  431.2 468.1 %reduce-scatter.12.cloned.1.call-start = ((), (), s32[]{:S(2)}) async-start(), calls=%async_computation.11 | async-start | bytes 1769472 | tf_op jit(solution)/shard_map/reduce_scatter | solution.py:259
  436.3 519.1 %reduce-scatter.14.cloned.1.call-start = ((), (), s32[]{:S(2)}) async-start(), calls=%async_computation.12 | async-start | bytes 5308416 | tf_op jit(solution)/shard_map/reduce_scatter | solution.py:261
  444.4 568.9 %reduce-scatter.8.cloned.1.call-start = ((), (), s32[]{:S(2)}) async-start(), calls=%async_computation.9 | async-start | bytes 5308416 | tf_op jit(solution)/shard_map/reduce_scatter | solution.py:257
  450.2 620.8 %reduce-scatter.10.cloned.1.call-start = ((), (), s32[]{:S(2)}) async-start(), calls=%async_computation.10 | async-start | bytes 5308416 | tf_op jit(solution)/shard_map/reduce_scatter | solution.py:258
  456.0 400.0 %copy-start.2 = (bf16[1024,1536]{1,0:T(8,128)(2,1)S(1)}, bf16[1024,1536]{1,0:T(8,128)(2,1)}, u32[]{:S(2)}) copy-start(bf16[1024,1536]{1,0:T(8,128)(2,1)} %param.22) | copy-start | bytes 9437188
  456.0 400.0 %copy-start.52 = (f32[1536]{0:T(1024)S(1)}, f32[1536]{0:T(1024)}, u32[]{:S(2)}) copy-start(f32[1536]{0:T(1024)} %param.23) | copy-start | bytes 18436
  456.0 400.0 %copy-start.56 = (f32[1024]{0:T(1024)S(1)}, f32[1024]{0:T(1024)}, u32[]{:S(2)}) copy-start(f32[1024]{0:T(1024)} %copy-done.55) | copy-start | bytes 12292
  (57 other events, 219.8 us)
Sparse Core Ops, SparseCore 0:
  9.6 29.9 all-gather.6
  41.1 23.6 all-gather.8
  66.4 24.0 all-gather.10
  334.0 49.6 all-reduce.13
  386.7 36.3 reduce-scatter.15
  431.3 424.6 all-reduce.15
  859.9 37.7 reduce-scatter.11
  901.7 53.7 reduce-scatter.13
  959.5 53.7 reduce-scatter.7
  1017.2 53.7 reduce-scatter.9
where the time goes:
time: 1090 us; the launch traced here: 1080 us
  waiting for transfers between devices  587 us (54%)
  matrix products  181 us (17%)
  other arithmetic  106 us (10%)
  local copies, waits for them, and re-layouts  91.8 us (8%)
  blocking collectives  89.3 us (8%)
  between operations  16.3 us (1%)
    psum x1, waiting for transfers between devices, shards(): out_total = lax.psum(out_part, 'tensor')  397 us
    reduce_scatter x1, waiting for transfers between devices, shards(): lax.psum_scatter(grad_w_z, ('shard', 'context'), scatter_dimension=0, til...  57.8 us
    reduce_scatter x1, waiting for transfers between devices, shards(): lax.psum_scatter(grad_w_x, ('shard', 'context'), scatter_dimension=0, til...  57.7 us
    reduce_scatter x1, waiting for transfers between devices, shards(): lax.psum_scatter(grad_w_out, ('shard', 'context'), scatter_dimension=1, t...  56.2 us
    dot_general x3, matrix products, group_output(): jnp.einsum('chts,cshp->cthp', decay * scores[:, None], x_step, precision=...  47.5 us
    psum x1, blocking collectives, shards(): lax.psum((grad_norm_gain, grad_conv_weight[:, :local_inner], grad_conv_bi...  25.9 us
  transfers between devices with their start and end apart: 12, of which 6 were waited for; matrix products, arithmetic and copies ran while one was open for 21% of the time, Pallas kernels for 0%

commit v1 on v0

--- a/solution.py
+++ b/solution.py
@@ -10,6 +10,11 @@
 GROUP = 256
 epsilon = 1e-05
 precise = lax.Precision.HIGHEST
+
+
+def _serve_boxes(xin, mesh_dim="tensor"):
+    reached = lax.all_gather(xin, axis_name=mesh_dim).sum(axis=0)
+    return reached
 
 
 def shifted(shard, axis, by):
@@ -181,7 +186,7 @@
     gate_inverse = lax.rsqrt(square_sum[:, None] / inner_width + epsilon)
     gated_out = (gated * gate_inverse * gate_gain).astype(jnp.bfloat16)
     out_part = jnp.dot(gated_out, full_out, preferred_element_type=jnp.float32)
-    out_total = lax.psum(out_part, "tensor")
+    out_total = _serve_boxes(out_part)
     block_output = (x_float + out_total).astype(jnp.bfloat16)
     grad_gated_out = jnp.einsum(
         "td,kd->tk", out_cotangent, full_out, preferred_element_type=jnp.float32

time: 1090 us -> 1310 us (1.20)
  waiting for transfers between devices: 587 us -> 789 us
  other arithmetic: 106 us -> 120 us
    all_gather x0 -> x1, waiting for transfers between devices: none -> 391 us  [_serve_boxes(): reached = lax.all_gather(xin, axis_name=mesh_dim).sum(axis=0)]
    psum x1, waiting for transfers between devices: 397 us -> 186 us  [shards(): lax.psum(partial_normed, 'tensor')]
    reduce_scatter x1, waiting for transfers between devices: 0.01 us -> 18 us  [shards(): lax.psum_scatter(grad_w_bc, ('shard', 'context'), scatter_dimension=0, ti...]
    reduce_sum x0 -> x1, other arithmetic: none -> 13.3 us  [_serve_boxes(): reached = lax.all_gather(xin, axis_name=mesh_dim).sum(axis=0)]
  transfers between devices with their start and end apart: 12 -> 13, of which waited for: 6 -> 8; matrix products, arithmetic and copies ran while one was open for 21% -> 18% of each run, Pallas kernels for 0% -> 0%
where the time goes in v1:
time: 1310 us; the launch traced here: 1300 us
  waiting for transfers between devices  789 us (60%)
  matrix products  184 us (14%)
  other arithmetic  120 us (9%)
  local copies, waits for them, and re-layouts  93.5 us (7%)
  blocking collectives  88.9 us (7%)
  between operations  16 us (1%)
    all_gather x1, waiting for transfers between devices, _serve_boxes(): reached = lax.all_gather(xin, axis_name=mesh_dim).sum(axis=0)  391 us
    psum x1, waiting for transfers between devices, shards(): lax.psum(partial_normed, 'tensor')  186 us
    reduce_scatter x1, waiting for transfers between devices, shards(): lax.psum_scatter(grad_w_out, ('shard', 'context'), scatter_dimension=1, t...  57.8 us
    reduce_scatter x1, waiting for transfers between devices, shards(): lax.psum_scatter(grad_w_x, ('shard', 'context'), scatter_dimension=0, til...  57.8 us
    reduce_scatter x1, waiting for transfers between devices, shards(): lax.psum_scatter(grad_w_z, ('shard', 'context'), scatter_dimension=0, til...  57.7 us
    dot_general x3, matrix products, group_output(): jnp.einsum('chts,cshp->cthp', decay * scores[:, None], x_step, precision=...  47.4 us
  transfers between devices with their start and end apart: 13, of which 8 were waited for; matrix products, arithmetic and copies ran while one was open for 18% of the time, Pallas kernels for 0%

profile of v1, /device:TPU:0, one launch (start us, length us, event | category | flops | bytes accessed | tf_op | source)
XLA Modules:
  0.0 1298.9 jit_solution(2627003078814106697)
XLA Ops:
  12.7 6.3 all_gather.43
  27.6 12.3 all_gather.42
  46.7 4.9 all-reduce.8
  52.2 4.4 convolution_convert_fusion
  57.7 4.2 collective-permute-start
  73.4 5.4 fusion.39
  82.8 5.2 reshape.251
  92.1 6.4 fusion.53
  99.8 7.6 while.59
  115.7 10.9 all-gather.1
  132.8 14.6 %bitcast_add_fusion.4 = f32[4,256,12,64]{1,3,2,0:T(8,128)S(1)} fusion(f32[4,256,12,64]{1,3,2,0:T(8,128)S(1)} %fusion.67, f32[4,256,256]{2,1,0:T(8,128)S(1)} %fusion.129, f32[4,12,256]{2,1,0:T(8,128)S(1)} %copy-done.32, pred[256,256]{1,0:T(8,128)(4,1)S(1)} %copy-done.52, f32[4,256,12,64]{1,0,3,2:T(4,128)S(1)} %copy-done.6, f32[4,256,12]{1,2,0:T(8,128)S(1)} %copy-done.42, ...), kind=kOutput, calls=%fused_computation.75 | convolution fusion | flops 2430861312 | bytes 10698752 | tf_op jit(solution)/shard_map/chts,cshp->cthp/dot_general | solution.py:89
  151.8 7.9 multiply_reduce_fusion.10
  159.7 11.7 psum.91
  171.4 8.7 multiply_reduce_fusion.4
  180.1 8.5 psum.92
  188.6 8.4 multiply_reduce_fusion.5
  200.0 7.0 multiply_reduce_fusion.11
  209.4 5.1 mul.624
  214.5 4.7 fusion.86
  219.2 8.8 all-gather.3
  229.9 14.8 %while.60 = (s32[]{:T(128)}, f32[12,64,128]{2,1,0:T(8,128)S(1)}, f32[4,12,64,128]{3,2,1,0:T(8,128)}, f32[4,12]{1,0:T(4,128)}, f32[4,12,1,1]{1,3,2,0:T(1,128)}, /...) while((s32[]{:T(128)}, f32[12,64,128]{2,1,0:T(8,128)S(1)}, ...), condition=%wide.region_13.14_spmd.clone, body=%wide.region_12.13_spmd.clone.sunk | while | flops 393219 | bytes 1967968 | solution.py:71
  248.6 18.8 %while.58 = (s32[]{:T(128)}, f32[12,64,128]{2,1,0:T(8,128)S(1)}, f32[4,12]{1,0:T(4,128)}, f32[4,12,64,128]{3,2,1,0:T(8,128)}, f32[4,12,64,128]{3,2,1,0:T(8,128)}...) while((s32[]{:T(128)}, f32[12,64,128]{2,1,0:T(8,128)S(1)}, ...), condition=%wide.region_16.17_spmd, body=%wide.region_14.16_spmd.sunk | while | flops 393219 | bytes 2359869 | solution.py:71
  267.3 6.0 multiply_reduce_fusion.6
  273.4 5.3 fusion.83
  278.7 20.5 %fusion.60 = (f32[4,12,256]{2,1,0:T(8,128)S(1)}, f32[4,12,256]{2,1,0:T(8,128)}, f32[4,256,256]{2,1,0:T(8,128)S(1)}) fusion(f32[4,12,256]{2,1,0:T(8,128)S(1)} %copy-done.33, f32[4,256,256]{2,1,0:T(8,128)S(1)} %copy-done.39, pred[256,256]{1,0:T(8,128)(4,1)S(1)} %copy-done.53, f32[4,256,12,64]{1,0,3,2:T(4,128)S(1)} %copy-done.7, ...), kind=kOutput, calls=%fused_computation.106 | convolution fusion | flops 2463604736 | bytes 8650752 | tf_op jit(solution)/shard_map/transpose(jvp(chts,cshp->cthp))/dot_general | solution.py:89
  299.2 6.2 fusion.80
  308.6 12.4 bitcast_add_fusion.3
  335.4 9.9 reduce-window.16
  363.7 7.7 fusion.130
  371.4 11.9 all-reduce.13.cloned.1.call-done
  383.3 13.0 %multiply_reduce_fusion.3 = (f32[1024]{0:T(1024)S(1)}, f32[1024]{0:T(1024)S(1)}, f32[1024]{0:T(1024)S(1)}, f32[1024]{0:T(1024)S(1)}, f32[1024]{0:T(1024)S(1)}, /*index=5*/f32[1024,1024]{0,1:T(8,128)S(1)}) fusion(f32[1027,1024]{0,1:T(8,128)} %copy-done, f32[1024,1024]{0,1:T(8,128)} %get-tuple-element.404, f32[1024,256]{0,1:T(8,128)} %all-reduce.13.cloned.1.call-done, ...), kind=kLoop, calls=%fused_computation.65 | loop fusion | flops 18869248 | bytes 29380608 | tf_op jit(solution)/shard_map/reduce_sum | solution.py:227
  402.3 9.7 pad_add_fusion
  412.0 6.8 collective-permute-done.1
  423.4 7.8 add_add_fusion
  433.1 6.5 fusion.121
  444.7 7.8 fusion.120
  452.8 5.8 fusion.131
  458.6 5.7 fusion.77
  467.1 185.6 %all-reduce.15.cloned.1.call-done = f32[1024,1536]{1,0:T(8,128)} async-done(((f32[1024,1536]{1,0:T(8,128)}), f32[1024,1536]{1,0:T(8,128)}) %all-reduce.15.cloned.1.call-update) | async-done | bytes 6291472 | tf_op jit(solution)/shard_map/psum | solution.py:243
  652.7 8.7 fusion.27
  661.4 25.5 %all-reduce.9 = (f32[1536]{0:T(1024)}, f32[4,768]{1,0:T(4,128)}, f32[768]{0:T(1024)}, f32[4,256]{1,0:T(4,128)}, f32[256]{0:T(256)}, /*index=5*/f32[12]{0:T(128)}, f32[12]{0:T(128)}, f32[12]{0:T(128)}, f32[768]{0:T(1024)}) all-reduce(f32[1536]{0:T(1024)S(1)} %get-tuple-element.332, ...), channel_id=1, replica_groups=mesh['shard'=4,'context'=2,'tensor'=4] {'shard','context'}, use_global_device_ids=true, to_apply=%region_38.39 | all-reduce | flops 7460 | bytes 59680 | tf_op jit(solution)/shard_map/psum | solution.py:278
  686.9 391.5 %all-gather.15.cloned.1.call-done = f32[4096,1536]{1,0:T(8,128)} async-done(((f32[1024,1536]{1,0:T(8,128)}), f32[4096,1536]{1,0:T(8,128)}) %all-gather.15.cloned.1.call-update) | async-done | bytes 25165840 | tf_op jit(solution)/shard_map/all_gather | solution.py:16
  1078.4 13.3 %reduce_sum.290 = f32[1024,1536]{1,0:T(8,128)} reduce(f32[4,1024,1536]{2,1,0:T(8,128)} %bitcast.216, f32[]{:T(128)} %constant.135.clone.1), dimensions={0}, to_apply=%region_9.10 | reduce | flops 4718592 | bytes 31457284 | tf_op jit(solution)/shard_map/reduce_sum | solution.py:16
  1091.7 9.1 fusion.22
  1100.8 18.0 %reduce-scatter.12.cloned.1.call-done = f32[192,256]{1,0:T(8,128)} async-done(((f32[1536,256]{1,0:T(8,128)}), f32[192,256]{1,0:T(8,128)}) %reduce-scatter.12.cloned.1.call-update) | async-done | bytes 196624 | tf_op jit(solution)/shard_map/reduce_scatter | solution.py:264
  1118.8 57.8 %reduce-scatter.14.cloned.1.call-done = f32[768,192]{0,1:T(8,128)} async-done(((f32[768,1536]{0,1:T(8,128)}), f32[768,192]{0,1:T(8,128)}) %reduce-scatter.14.cloned.1.call-update) | async-done | bytes 589840 | tf_op jit(solution)/shard_map/reduce_scatter | solution.py:266
  1176.6 57.7 %reduce-scatter.8.cloned.1.call-done = f32[192,768]{1,0:T(8,128)} async-done(((f32[1536,768]{1,0:T(8,128)}), f32[192,768]{1,0:T(8,128)}) %reduce-scatter.8.cloned.1.call-update) | async-done | bytes 589840 | tf_op jit(solution)/shard_map/reduce_scatter | solution.py:262
  1234.3 57.8 %reduce-scatter.10.cloned.1.call-done = f32[192,768]{1,0:T(8,128)} async-done(((f32[1536,768]{1,0:T(8,128)}), f32[192,768]{1,0:T(8,128)}) %reduce-scatter.10.cloned.1.call-update) | async-done | bytes 589840 | tf_op jit(solution)/shard_map/reduce_scatter | solution.py:263
  (373 shorter events, 169.5 us)
Async XLA Ops:
  7.2 11.9 copy-start.1
  7.2 11.8 copy-start.88
  7.2 11.8 copy-start.50
  7.2 45.0 %all-gather.9.cloned.1.call-start = ((), (), s32[]{:S(2)}) async-start(), calls=%async_computation.5 | async-start | bytes 2949120 | tf_op jit(solution)/shard_map/all_gather | solution.py:146
  8.0 143.8 %all-gather.11.cloned.1.call-start = ((), (), s32[]{:S(2)}) async-start(), calls=%async_computation.6 | async-start | bytes 2949120 | tf_op jit(solution)/shard_map/all_gather | solution.py:145
  8.7 162.7 %all-gather.13.cloned.1.call-start = ((), (), s32[]{:S(2)}) async-start(), calls=%async_computation.7 | async-start | bytes 2949120 | tf_op jit(solution)/shard_map/all_gather | solution.py:149
  9.4 373.9 %all-reduce.13.cloned.1.call-start = ((), (), s32[]{:S(2)}) async-start(), calls=%async_computation.8 | async-start | bytes 2097152 | tf_op jit(solution)/shard_map/psum | solution.py:222
  26.5 19.9 %copy-start.84 = (f32[12]{0:T(128)}, f32[12]{0:T(128)S(1)}, u32[]{:S(2)}) copy-start(f32[12]{0:T(128)S(1)} %get-tuple-element.342) | copy-start | bytes 148
  27.6 16.9 %copy-start.70 = (f32[4,768]{1,0:T(4,128)S(1)}, f32[4,768]{1,0:T(4,128)}, u32[]{:S(2)}) copy-start(f32[4,768]{1,0:T(4,128)} %param.28) | copy-start | bytes 36868
  27.6 16.9 %copy-start.80 = (f32[4,256]{1,0:T(4,128)S(1)}, f32[4,256]{1,0:T(4,128)}, u32[]{:S(2)}) copy-start(f32[4,256]{1,0:T(4,128)} %param.30) | copy-start | bytes 12292
  27.6 17.5 %copy-start.90 = (u32[32]{0:T(128)S(1)}, u32[32]{0:T(128)}, u32[]{:S(2)}) copy-start(u32[32]{0:T(128)} %constant.163) | copy-start | bytes 388
  27.6 24.6 %copy-start.4 = (bf16[1024,1536]{1,0:T(8,128)(2,1)S(1)}, bf16[1024,1536]{1,0:T(8,128)(2,1)}, u32[]{:S(2)}) copy-start(bf16[1024,1536]{1,0:T(8,128)(2,1)} %copy-done.3) | copy-start | bytes 9437188
  45.2 28.2 %copy-start.58 = (f32[1,1024]{1,0:T(1,128)}, f32[1,1024]{1,0:T(1,128)S(1)}, u32[]{:S(2)}) copy-start(f32[1,1024]{1,0:T(1,128)S(1)} %get-tuple-element.422) | copy-start | bytes 12292
  52.2 9.7 copy-start.83
  52.2 13.3 %copy-start.87 = (f32[12]{0:T(128)S(1)}, f32[12]{0:T(128)}, u32[]{:S(2)}) copy-start(f32[12]{0:T(128)} %param.34) | copy-start | bytes 148
  57.7 12.9 collective-permute-start
  66.9 121.7 %copy-start.56 = (f32[768]{0:T(1024)}, f32[768]{0:T(1024)S(1)}, u32[]{:S(2)}) copy-start(f32[768]{0:T(1024)S(1)} %mul.593) | copy-start | bytes 9220
  107.5 20.1 %copy-start.76 = (f32[12]{0:T(128)S(1)}, f32[12]{0:T(128)}, u32[]{:S(2)}) copy-start(f32[12]{0:T(128)} %get-tuple-element.427) | copy-start | bytes 148
  115.7 14.3 %copy-start.23 = (f32[4,256,128,1]{2,1,3,0:T(8,128)S(1)}, f32[4,256,128,1]{2,1,3,0:T(8,128)}, u32[]{:S(2)}) copy-start(f32[4,256,128,1]{2,1,3,0:T(8,128)} %copy.238) | copy-start | bytes 1572868
  115.7 14.3 %copy-start.26 = (f32[4,12,64,128]{3,2,1,0:T(8,128)S(1)}, f32[4,12,64,128]{3,2,1,0:T(8,128)}, u32[]{:S(2)}) copy-start(f32[4,12,64,128]{3,2,1,0:T(8,128)} %get-tuple-element.280) | copy-start | bytes 4718596
  127.6 72.4 %copy-start.16 = (f32[12,64,128]{2,1,0:T(8,128)}, f32[12,64,128]{2,1,0:T(8,128)S(1)}, u32[]{:S(2)}) copy-start(f32[12,64,128]{2,1,0:T(8,128)S(1)} %fusion.102) | copy-start | bytes 1179652
  130.0 17.4 %copy-start.38 = (f32[4,256,256]{2,1,0:T(8,128)}, f32[4,256,256]{2,1,0:T(8,128)S(1)}, u32[]{:S(2)}) copy-start(f32[4,256,256]{2,1,0:T(8,128)S(1)} %fusion.129) | copy-start | bytes 3145732
  171.4 17.2 %copy-start.67 = (f32[1024]{0:T(1024)}, f32[1024]{0:T(1024)S(1)}, u32[]{:S(2)}) copy-start(f32[1024]{0:T(1024)S(1)} %add_rsqrt_fusion) | copy-start | bytes 12292
  214.5 15.4 %copy-start.9 = (f32[12,64,128]{2,1,0:T(8,128)S(1)}, f32[12,64,128]{2,1,0:T(8,128)}, u32[]{:S(2)}) copy-start(f32[12,64,128]{2,1,0:T(8,128)} %custom-call.1) | copy-start | bytes 1179652
  229.9 14.9 %copy-start.77 = (f32[12]{0:T(128)S(1)}, f32[12]{0:T(128)}, u32[]{:S(2)}) copy-start(f32[12]{0:T(128)} %get-tuple-element.427) | copy-start | bytes 148
  278.7 20.5 %copy-start.13 = (f32[4,12,64,128]{3,2,1,0:T(8,128)S(1)}, f32[4,12,64,128]{3,2,1,0:T(8,128)}, u32[]{:S(2)}) copy-start(f32[4,12,64,128]{3,2,1,0:T(8,128)} %get-tuple-element.662) | copy-start | bytes 4718596
  278.7 20.5 %copy-start.17 = (f32[12,64,128]{2,1,0:T(8,128)S(1)}, f32[12,64,128]{2,1,0:T(8,128)}, u32[]{:S(2)}) copy-start(f32[12,64,128]{2,1,0:T(8,128)} %copy-done.16) | copy-start | bytes 1179652
  278.7 20.5 %copy-start.43 = (f32[4,256,12]{1,2,0:T(8,128)S(1)}, f32[4,256,12]{1,2,0:T(8,128)}, u32[]{:S(2)}) copy-start(f32[4,256,12]{1,2,0:T(8,128)} %get-tuple-element.419) | copy-start | bytes 147460
  299.2 21.8 %copy-start.27 = (f32[4,256,256]{2,1,0:T(8,128)}, f32[4,256,256]{2,1,0:T(8,128)S(1)}, u32[]{:S(2)}) copy-start(f32[4,256,256]{2,1,0:T(8,128)S(1)} %get-tuple-element.331) | copy-start | bytes 3145732
  308.6 12.4 copy-start.22
  333.5 131.8 %reduce-scatter.16.cloned.1.call-start = ((), (), s32[]{:S(2)}) async-start(), calls=%async_computation.15 | async-start | bytes 884736
  363.3 289.4 %all-reduce.15.cloned.1.call-start = ((), (), s32[]{:S(2)}) async-start(), calls=%async_computation.9 | async-start | bytes 12582912 | tf_op jit(solution)/shard_map/psum | solution.py:243
  363.7 19.6 %copy-start.19 = (f32[1024,768]{0,1:T(8,128)S(1)}, f32[1024,768]{0,1:T(8,128)}, u32[]{:S(2)}) copy-start(f32[1024,768]{0,1:T(8,128)} %fusion.40) | copy-start | bytes 9437188
  383.3 13.0 %copy-start.59 = (f32[1,1024]{1,0:T(1,128)S(1)}, f32[1,1024]{1,0:T(1,128)}, u32[]{:S(2)}) copy-start(f32[1,1024]{1,0:T(1,128)} %copy-done.58) | copy-start | bytes 12292
  383.3 13.0 %copy-start.61 = (f32[1,1024]{1,0:T(1,128)S(1)}, f32[1,1024]{1,0:T(1,128)}, u32[]{:S(2)}) copy-start(f32[1,1024]{1,0:T(1,128)} %get-tuple-element.423) | copy-start | bytes 12292
  383.3 13.1 %copy-start.63 = (f32[1,1024]{1,0:T(1,128)S(1)}, f32[1,1024]{1,0:T(1,128)}, u32[]{:S(2)}) copy-start(f32[1,1024]{1,0:T(1,128)} %get-tuple-element.424) | copy-start | bytes 12292
  383.3 13.1 %copy-start.65 = (f32[1,1024]{1,0:T(1,128)S(1)}, f32[1,1024]{1,0:T(1,128)}, u32[]{:S(2)}) copy-start(f32[1,1024]{1,0:T(1,128)} %get-tuple-element.425) | copy-start | bytes 12292
  401.0 17.8 %collective-permute-start.1 = (f32[3,1024]{0,1:T(8,128)S(1)}, f32[3,1024]{0,1:T(8,128)S(1)}, u32[]{:S(2)}, u32[]{:S(2)}) collective-permute-start(f32[3,1024]{0,1:T(8,128)S(1)} %pad_add_fusion.1), channel_id=1, source_target_pairs={{4,0},{5,1},{6,2},{7,3},{12,8},{13,9},{14,10},{15,11},{20,16},{21,... | collective-permute-start | bytes 36872 | tf_op jit(solution)/shard_map/ppermute | solution.py:23
  412.0 11.4 copy-start.34
  431.2 647.2 %all-gather.15.cloned.1.call-start = ((), (), s32[]{:S(2)}) async-start(), calls=%async_computation.14 | async-start | bytes 31457280 | tf_op jit(solution)/shard_map/all_gather | solution.py:16
  439.5 679.3 %reduce-scatter.12.cloned.1.call-start = ((), (), s32[]{:S(2)}) async-start(), calls=%async_computation.12 | async-start | bytes 1769472 | tf_op jit(solution)/shard_map/reduce_scatter | solution.py:264
  444.6 732.0 %reduce-scatter.14.cloned.1.call-start = ((), (), s32[]{:S(2)}) async-start(), calls=%async_computation.13 | async-start | bytes 5308416 | tf_op jit(solution)/shard_map/reduce_scatter | solution.py:266
  452.5 781.8 %reduce-scatter.8.cloned.1.call-start = ((), (), s32[]{:S(2)}) async-start(), calls=%async_computation.10 | async-start | bytes 5308416 | tf_op jit(solution)/shard_map/reduce_scatter | solution.py:262
  458.6 833.5 %reduce-scatter.10.cloned.1.call-start = ((), (), s32[]{:S(2)}) async-start(), calls=%async_computation.11 | async-start | bytes 5308416 | tf_op jit(solution)/shard_map/reduce_scatter | solution.py:263
  464.3 188.4 %copy-start.2 = (bf16[1024,1536]{1,0:T(8,128)(2,1)S(1)}, bf16[1024,1536]{1,0:T(8,128)(2,1)}, u32[]{:S(2)}) copy-start(bf16[1024,1536]{1,0:T(8,128)(2,1)} %param.22) | copy-start | bytes 9437188
  464.3 188.4 %copy-start.51 = (f32[1536]{0:T(1024)S(1)}, f32[1536]{0:T(1024)}, u32[]{:S(2)}) copy-start(f32[1536]{0:T(1024)} %param.23) | copy-start | bytes 18436
  464.4 188.4 %copy-start.55 = (f32[1024]{0:T(1024)S(1)}, f32[1024]{0:T(1024)}, u32[]{:S(2)}) copy-start(f32[1024]{0:T(1024)} %copy-done.54) | copy-start | bytes 12292
  467.1 194.3 %copy-start.79 = (f32[768]{0:T(1024)S(1)}, f32[768]{0:T(1024)}, u32[]{:S(2)}) copy-start(f32[768]{0:T(1024)} %get-tuple-element.338) | copy-start | bytes 9220
  (56 other events, 210.2 us)
Sparse Core Ops, SparseCore 0:
  9.6 29.9 all-gather.8
  41.1 23.6 all-gather.10
  66.4 24.0 all-gather.12
  333.6 49.6 all-reduce.12
  386.3 36.3 reduce-scatter.15
  431.3 221.3 all-reduce.14
  654.3 424.0 all-gather.14
  1082.2 36.5 reduce-scatter.11
  1122.8 53.7 reduce-scatter.13
  1180.5 53.7 reduce-scatter.7
  1238.3 53.7 reduce-scatter.9
